TPU v7x, 32 devices: a whole 2x2x4 slice. The times are simulated.
32 devices in a mesh: rep: 4 (over x, core), row: 4 (over z), col: 2 (over y).
Axes of the slice: x: 2, y: 2, z: 4, core: 2. Of those that a mesh axis runs over, the one named last changes fastest.
Arguments:
- inputs: bfloat16 [4, 128, 6144], P('rep', 'col', 'row'), may hold values from -6 to 6
- w_in: bfloat16 [6144, 24576], P('row', ('rep', 'col')), may hold values from -0.078125 to 0.078125
- w_out: bfloat16 [24576, 6144], P(('rep', 'col'), 'row'), may hold values from -0.0390625 to 0.0390625
- cotangent: bfloat16 [4, 128, 6144], P('rep', 'col', 'row'), may hold values from -1536 to 1536
- counts: int32 [4], replicated, may hold values from 0 to 4, as said below
Outputs:
- block_output: bfloat16 [4, 128, 6144], P('rep', 'col', 'row')
- input_grad: bfloat16 [4, 128, 6144], P('rep', 'col', 'row')
- w_in_grad: float32 [6144, 24576], P('row', ('rep', 'col'))
- w_out_grad: float32 [24576, 6144], P(('rep', 'col'), 'row')
Inputs may be any that keep to these rules, and one draw needn't show every extreme that they name: Replica r completed its first counts[r] micro-batches; at least one replica completed all 4.
All inputs are finite; a program needn't handle non-finite values.
Results may differ from a plain program's by a relative error of at most 0.015.
Values may be sent and summed in bfloat16 or wider, within the bound.
A program may use at most 192 MiB of HBM per device.

v0:
```python
import jax
import jax.numpy as jnp
from jax import lax
from jax.sharding import PartitionSpec as P

MBT = 32
root_coef = 0.7978845608028654
cubic_coef = 0.044715


def gelu_tanh(values):
    inner = root_coef * (values + cubic_coef * values * values * values)
    return 0.5 * values * (1.0 + jnp.tanh(inner))


def gelu_slope(values):
    inner = root_coef * (values + cubic_coef * values * values * values)
    tangent = jnp.tanh(inner)
    return 0.5 * (1.0 + tangent) + 0.5 * values * (1.0 - tangent * tangent) * root_coef * (
        1.0 + 3.0 * cubic_coef * values * values
    )


def right_product(left, right):
    return lax.dot_general(
        left, right, (((1,), (1,)), ((), ())), preferred_element_type=jnp.float32
    )


def first_product(left, right):
    return lax.dot_general(
        left, right, (((0,), (0,)), ((), ())), preferred_element_type=jnp.float32
    )


def body(inputs, w_in, w_out, cotangent, counts):
    rows_local = inputs.shape[1]
    width_local = inputs.shape[2]
    tokens_local = inputs.reshape(rows_local, width_local)
    replicas = lax.axis_size("rep")
    replica_index = lax.axis_index("rep")
    column_index = lax.axis_index("col")
    own_count = jnp.sum(jnp.where(jnp.arange(replicas) == replica_index, counts, 0))
    token_total = (MBT * jnp.sum(counts)).astype(jnp.float32)
    positions = column_index * rows_local + jnp.arange(rows_local, dtype=jnp.int32)
    kept_mask = (positions // MBT < own_count).astype(jnp.float32)
    scaled = (
        cotangent.reshape(rows_local, width_local).astype(jnp.float32)
        * kept_mask[:, None]
        / token_total
    ).astype(jnp.bfloat16)
    tokens_all = lax.all_gather(tokens_local, ("rep", "col"), axis=0, tiled=True)
    scaled_all = lax.all_gather(scaled, ("rep", "col"), axis=0, tiled=True)
    partial_hidden = jnp.dot(tokens_all, w_in, preferred_element_type=jnp.float32)
    hidden = lax.psum_scatter(
        partial_hidden.astype(jnp.bfloat16), "row", scatter_dimension=0, tiled=True
    ).astype(jnp.float32)
    slope_terms = right_product(scaled_all, w_out)
    slope_sum = lax.psum_scatter(
        slope_terms.astype(jnp.bfloat16), "row", scatter_dimension=0, tiled=True
    ).astype(jnp.float32)
    active_share = gelu_tanh(hidden).astype(jnp.bfloat16)
    activated = lax.all_gather(active_share, "row", axis=0, tiled=True)
    grad_share = (slope_sum * gelu_slope(hidden)).astype(jnp.bfloat16)
    hidden_grad = lax.all_gather(grad_share, "row", axis=0, tiled=True)
    output_terms = jnp.dot(activated, w_out, preferred_element_type=jnp.float32)
    output_local = lax.psum_scatter(
        output_terms.astype(jnp.bfloat16), ("rep", "col"), scatter_dimension=0, tiled=True
    ).astype(jnp.float32)
    block_output = (tokens_local.astype(jnp.float32) + output_local).astype(jnp.bfloat16)
    w_out_grad = first_product(activated, scaled_all)
    back_terms = right_product(hidden_grad, w_in)
    back_local = lax.psum_scatter(
        back_terms.astype(jnp.bfloat16), ("rep", "col"), scatter_dimension=0, tiled=True
    ).astype(jnp.float32)
    input_grad = (scaled.astype(jnp.float32) + back_local).astype(jnp.bfloat16)
    w_in_grad = first_product(tokens_all, hidden_grad)
    return (
        block_output.reshape(1, rows_local, width_local),
        input_grad.reshape(1, rows_local, width_local),
        w_in_grad,
        w_out_grad,
    )


def solution(mesh):
    placed = (
        P("rep", "col", "row"),
        P("row", ("rep", "col")),
        P(("rep", "col"), "row"),
        P("rep", "col", "row"),
        P(),
    )
    return jax.shard_map(
        body,
        mesh=mesh,
        in_specs=placed,
        out_specs=(
            P("rep", "col", "row"),
            P("rep", "col", "row"),
            P("row", ("rep", "col")),
            P(("rep", "col"), "row"),
        ),
        check_vma=False,
    )
```

profile of v0, /device:TPU:0, one launch (start us, length us, event | category | flops | bytes accessed | tf_op | source)
XLA Modules:
  0.0 415.8 jit_solution(2729077798957875447)
XLA Ops:
  7.2 0.0 all-gather.8.cloned.1.call-start
  7.2 1.3 fusion.18
  9.2 0.7 compare_convert_fusion
  9.8 1.7 fusion.14
  11.6 0.0 all-gather.12.cloned.1.call-start
  11.6 0.7 all-gather.12.cloned.1.call-update
  12.3 0.0 reduce-scatter.9.cloned.1.call-start
  12.4 27.6 %all-gather.8.cloned.1.call-done = bf16[512,1536]{1,0:T(8,128)(2,1)} async-done(((bf16[64,1536]{1,0:T(8,128)(2,1)}), bf16[512,1536]{1,0:T(8,128)(2,1)}) %all-gather.8.cloned.1.call-update) | async-done | bytes 1572880 | tf_op jit(solution)/shard_map/all_gather | solution.py:53
  40.0 9.3 %convolution_convert_fusion = bf16[512,3072]{1,0:T(8,128)(2,1)} fusion(bf16[512,1536]{1,0:T(8,128)(2,1)} %all-gather.8.cloned.1.call-done, bf16[3072,1536]{1,0:T(8,128)(2,1)} %param.7), kind=kOutput, calls=%fused_computation.1 | convolution fusion | flops 4833411072 | bytes 14155776 | tf_op jit(solution)/shard_map/dot_general | solution.py:25
  49.3 0.0 reduce-scatter.9.cloned.1.call-update
  49.3 0.0 reduce-scatter.5.cloned.1.call-start
  49.4 18.1 %all-gather.12.cloned.1.call-done = bf16[1,512,1536]{2,1,0:T(8,128)(2,1)} async-done(((bf16[1,64,1536]{2,1,0:T(8,128)(2,1)}), bf16[1,512,1536]{2,1,0:T(8,128)(2,1)}) %all-gather.12.cloned.1.call-update) | async-done | bytes 1572880 | tf_op jit(solution)/shard_map/all_gather | solution.py:52
  67.5 9.2 %convolution_convert_fusion.1 = bf16[512,3072]{1,0:T(8,128)(2,1)} fusion(bf16[1536,3072]{1,0:T(8,128)(2,1)} %param.6, bf16[1,512,1536]{2,1,0:T(8,128)(2,1)} %all-gather.12.cloned.1.call-done), kind=kOutput, calls=%fused_computation.2 | convolution fusion | flops 4833411072 | bytes 14155776 | tf_op jit(solution)/shard_map/dot_general | solution.py:54
  76.7 0.0 all-gather.6.cloned.1.call-start
  76.8 54.0 %reduce-scatter.9.cloned.1.call-done = bf16[128,3072]{1,0:T(8,128)(2,1)} async-done(((bf16[512,3072]{1,0:T(8,128)(2,1)}), bf16[128,3072]{1,0:T(8,128)(2,1)}) %reduce-scatter.9.cloned.1.call-update) | async-done | bytes 786448 | tf_op jit(solution)/shard_map/reduce_scatter | solution.py:59
  130.8 63.1 %reduce-scatter.5.cloned.1.call-done = bf16[128,3072]{1,0:T(8,128)(2,1)} async-done(((bf16[512,3072]{1,0:T(8,128)(2,1)}), bf16[128,3072]{1,0:T(8,128)(2,1)}) %reduce-scatter.5.cloned.1.call-update) | async-done | bytes 786448 | tf_op jit(solution)/shard_map/reduce_scatter | solution.py:55
  193.9 3.7 fusion.7
  197.6 0.0 all-gather.6.cloned.1.call-update
  197.6 0.0 all-gather.10.cloned.1.call-start
  197.7 0.5 all-gather.10.cloned.1.call-update
  198.2 0.0 reduce-scatter.7.cloned.1.call-start
  198.2 62.9 %all-gather.6.cloned.1.call-done = bf16[512,3072]{1,0:T(8,128)(2,1)} async-done(((bf16[128,3072]{1,0:T(8,128)(2,1)}), bf16[512,3072]{1,0:T(8,128)(2,1)}) %all-gather.6.cloned.1.call-update) | async-done | bytes 3145744 | tf_op jit(solution)/shard_map/all_gather | solution.py:63
  261.1 10.3 %convolution_convert_fusion.3 = bf16[512,1536]{1,0:T(8,128)(2,1)} fusion(bf16[512,3072]{1,0:T(8,128)(2,1)} %all-gather.6.cloned.1.call-done, bf16[3072,1536]{1,0:T(8,128)(2,1)} %param.7), kind=kOutput, calls=%fused_computation.11 | convolution fusion | flops 4832624640 | bytes 14155776 | tf_op jit(solution)/shard_map/dot_general | solution.py:66
  271.4 0.2 reduce-scatter.11.cloned.1.call-start
  271.6 53.6 %all-gather.10.cloned.1.call-done = bf16[512,3072]{1,0:T(8,128)(2,1)} async-done(((bf16[128,3072]{1,0:T(8,128)(2,1)}), bf16[512,3072]{1,0:T(8,128)(2,1)}) %all-gather.10.cloned.1.call-update) | async-done | bytes 3145744 | tf_op jit(solution)/shard_map/all_gather | solution.py:65
  325.2 10.5 %convolution_convert_fusion.2 = bf16[512,1536]{1,0:T(8,128)(2,1)} fusion(bf16[512,3072]{1,0:T(8,128)(2,1)} %all-gather.10.cloned.1.call-done, bf16[1536,3072]{1,0:T(8,128)(2,1)} %param.6), kind=kOutput, calls=%fused_computation.10 | convolution fusion | flops 4832624640 | bytes 14155776 | tf_op jit(solution)/shard_map/dot_general | solution.py:25
  335.7 11.0 %convolution_bitcast_fusion = f32[1536,3072]{0,1:T(8,128)} fusion(bf16[512,3072]{1,0:T(8,128)(2,1)S(1)} %copy-done.3, bf16[1,512,1536]{2,1,0:T(8,128)(2,1)} %all-gather.12.cloned.1.call-done), kind=kOutput, calls=%fused_computation | convolution fusion | flops 4831838208 | bytes 23592960 | tf_op jit(solution)/shard_map/dot_general | solution.py:31
  346.8 19.0 %copy.9 = f32[1536,3072]{1,0:T(8,128)} copy(f32[1536,3072]{0,1:T(8,128)} %convolution_bitcast_fusion) | data formatting | bytes 37748736
  365.8 11.0 %fusion.19 = f32[3072,1536]{1,0:T(8,128)} fusion(bf16[512,3072]{1,0:T(8,128)(2,1)S(1)} %copy-done.2, bf16[512,1536]{1,0:T(8,128)(2,1)} %all-gather.8.cloned.1.call-done), kind=kOutput, calls=%fused_computation.40 | convolution fusion | flops 4831838208 | bytes 23592960 | tf_op jit(solution)/shard_map/dot_general | solution.py:31
  376.8 1.7 fusion.17
  378.4 28.8 %reduce-scatter.11.cloned.1.call-done = bf16[64,1536]{1,0:T(8,128)(2,1)} async-done(((bf16[512,1536]{1,0:T(8,128)(2,1)}), bf16[64,1536]{1,0:T(8,128)(2,1)}) %reduce-scatter.11.cloned.1.call-update) | async-done | bytes 196624 | tf_op jit(solution)/shard_map/reduce_scatter | solution.py:73
  407.2 1.7 fusion.16
  (13 shorter events, 0.1 us)
Async XLA Ops:
  7.2 32.9 %all-gather.8.cloned.1.call-start = ((), (), s32[]{:S(2)}) async-start(), calls=%async_computation.7 | async-start | bytes 1769472 | tf_op jit(solution)/shard_map/all_gather | solution.py:53
  11.6 55.9 %all-gather.12.cloned.1.call-start = ((), (), s32[]{:S(2)}) async-start(), calls=%async_computation.11 | async-start | bytes 1769472 | tf_op jit(solution)/shard_map/all_gather | solution.py:52
  12.3 118.5 %reduce-scatter.9.cloned.1.call-start = ((), (), s32[]{:S(2)}) async-start(), calls=%async_computation.8 | async-start | bytes 3932160 | tf_op jit(solution)/shard_map/reduce_scatter | solution.py:59
  49.3 144.6 %reduce-scatter.5.cloned.1.call-start = ((), (), s32[]{:S(2)}) async-start(), calls=%async_computation.4 | async-start | bytes 3932160 | tf_op jit(solution)/shard_map/reduce_scatter | solution.py:55
  76.7 184.4 %all-gather.6.cloned.1.call-start = ((), (), s32[]{:S(2)}) async-start(), calls=%async_computation.5 | async-start | bytes 3932160 | tf_op jit(solution)/shard_map/all_gather | solution.py:63
  197.6 127.6 %all-gather.10.cloned.1.call-start = ((), (), s32[]{:S(2)}) async-start(), calls=%async_computation.9 | async-start | bytes 3932160 | tf_op jit(solution)/shard_map/all_gather | solution.py:65
  198.2 178.6 %reduce-scatter.7.cloned.1.call-start = ((), (), s32[]{:S(2)}) async-start(), calls=%async_computation.6 | async-start | bytes 1769472 | tf_op jit(solution)/shard_map/reduce_scatter | solution.py:67
  271.4 135.8 %reduce-scatter.11.cloned.1.call-start = ((), (), s32[]{:S(2)}) async-start(), calls=%async_computation.10 | async-start | bytes 1769472 | tf_op jit(solution)/shard_map/reduce_scatter | solution.py:73
  325.2 10.5 %copy-start.3 = (bf16[512,3072]{1,0:T(8,128)(2,1)S(1)}, bf16[512,3072]{1,0:T(8,128)(2,1)}, u32[]{:S(2)}) copy-start(bf16[512,3072]{1,0:T(8,128)(2,1)} %all-gather.10.cloned.1.call-done) | copy-start | bytes 9437188
  346.8 19.0 %copy-start.2 = (bf16[512,3072]{1,0:T(8,128)(2,1)S(1)}, bf16[512,3072]{1,0:T(8,128)(2,1)}, u32[]{:S(2)}) copy-start(bf16[512,3072]{1,0:T(8,128)(2,1)} %all-gather.6.cloned.1.call-done) | copy-start | bytes 9437188
  365.8 11.0 %copy-start = (bf16[1,64,1536]{2,1,0:T(8,128)(2,1)S(1)}, bf16[1,64,1536]{2,1,0:T(8,128)(2,1)}, u32[]{:S(2)}) copy-start(bf16[1,64,1536]{2,1,0:T(8,128)(2,1)} %param.5) | copy-start | bytes 589828
  365.8 41.4 %copy-start.1 = (bf16[1,64,1536]{2,1,0:T(8,128)(2,1)S(1)}, bf16[1,64,1536]{2,1,0:T(8,128)(2,1)}, u32[]{:S(2)}) copy-start(bf16[1,64,1536]{2,1,0:T(8,128)(2,1)} %param.8) | copy-start | bytes 589828
Sparse Core Ops, SparseCore 0:
  11.7 28.2 all-gather.7
  41.9 25.5 all-gather.11
  70.4 60.3 reduce-scatter.8
  133.5 60.3 reduce-scatter.4
  197.7 63.3 all-gather.5
  263.1 62.0 all-gather.9
  328.5 36.9 reduce-scatter.6
  368.8 38.3 reduce-scatter.10
where the time goes:
time: 416 us
  waiting for transfers between devices  309 us (74%)
  matrix products  61.2 us (15%)
  local copies, waits for them, and re-layouts  19 us (5%)
  between operations  14.8 us (4%)
  other arithmetic  10.8 us (3%)
    reduce_scatter x1, waiting for transfers between devices, body(): lax.psum_scatter(partial_hidden.astype(jnp.bfloat16), 'row', scatter_dime...  63.1 us
    all_gather x1, waiting for transfers between devices, body(): activated = lax.all_gather(active_share, 'row', axis=0, tiled=True)  62.9 us
    reduce_scatter x1, waiting for transfers between devices, body(): lax.psum_scatter(slope_terms.astype(jnp.bfloat16), 'row', scatter_dimensi...  54 us
    all_gather x1, waiting for transfers between devices, body(): hidden_grad = lax.all_gather(grad_share, 'row', axis=0, tiled=True)  53.6 us
    reduce_scatter x1, waiting for transfers between devices, body(): lax.psum_scatter(back_terms.astype(jnp.bfloat16), ('rep', 'col'), scatter...  28.8 us
    all_gather x1, waiting for transfers between devices, body(): scaled_all = lax.all_gather(scaled, ('rep', 'col'), axis=0, tiled=True)  27.6 us
    dot_general x2, matrix products, first_product(): lax.dot_general(left, right, (((0,), (0,)), ((), ())), preferred_element_...  22 us
    dot_general x2, matrix products, right_product(): lax.dot_general(left, right, (((1,), (1,)), ((), ())), preferred_element_...  19.7 us
  transfers between devices with their start and end apart: 8, of which 7 were waited for; matrix products, arithmetic and copies ran while one was open for 20% of the time, Pallas kernels for 0%

commit v1 on v0

--- a/solution.py
+++ b/solution.py
@@ -62,7 +62,12 @@
     active_share = gelu_tanh(hidden).astype(jnp.bfloat16)
     activated = lax.all_gather(active_share, "row", axis=0, tiled=True)
     grad_share = (slope_sum * gelu_slope(hidden)).astype(jnp.bfloat16)
-    hidden_grad = lax.all_gather(grad_share, "row", axis=0, tiled=True)
+    ring = [grad_share]
+    for hop in range(3):
+        ring.append(lax.ppermute(ring[-1], "row", [(dev, (dev + 1) % 4) for dev in range(4)]))
+    hidden_grad = jnp.roll(
+        jnp.concatenate(ring[::-1], axis=0), (lax.axis_index("row") + 1) * ring[0].shape[0], axis=0
+    )
     output_terms = jnp.dot(activated, w_out, preferred_element_type=jnp.float32)
     output_local = lax.psum_scatter(
         output_terms.astype(jnp.bfloat16), ("rep", "col"), scatter_dimension=0, tiled=True

time: 416 us -> 399 us (0.959)
  waiting for transfers between devices: 309 us -> 289 us
    ppermute x0 -> x3, waiting for transfers between devices: none -> 66.7 us  [body(): lax.ppermute(ring[-1], 'row', [(dev, (dev + 1) % 4) for dev in range(4)])]
    all_gather x1 -> x0, waiting for transfers between devices: 53.6 us -> none  [body(): hidden_grad = lax.all_gather(grad_share, 'row', axis=0, tiled=True)]
    all_gather x1, waiting for transfers between devices: 62.9 us -> 30.7 us  [body(): activated = lax.all_gather(active_share, 'row', axis=0, tiled=True)]
    reduce_scatter x1, waiting for transfers between devices: 28.8 us -> 0.01 us  [body(): lax.psum_scatter(back_terms.astype(jnp.bfloat16), ('rep', 'col'), scatter...]
    reduce_scatter x1, waiting for transfers between devices: 0.01 us -> 27.5 us  [body(): lax.psum_scatter(output_terms.astype(jnp.bfloat16), ('rep', 'col'), scatt...]
    unnamed x9 -> x18, local copies, waits for them, and re-layouts: 19 us -> 21.9 us
  transfers between devices with their start and end apart: 8 -> 10, of which waited for: 7 -> 9; matrix products, arithmetic and copies ran while one was open for 20% -> 21% of each run, Pallas kernels for 0% -> 0%
where the time goes in v1:
time: 399 us; the launch traced here: 398 us
  waiting for transfers between devices  289 us (72%)
  matrix products  60.8 us (15%)
  local copies, waits for them, and re-layouts  21.9 us (5%)
  between operations  14.9 us (4%)
  other arithmetic  10.5 us (3%)
    ppermute x3, waiting for transfers between devices, body(): lax.ppermute(ring[-1], 'row', [(dev, (dev + 1) % 4) for dev in range(4)])  66.7 us
    reduce_scatter x1, waiting for transfers between devices, body(): lax.psum_scatter(partial_hidden.astype(jnp.bfloat16), 'row', scatter_dime...  63.1 us
    reduce_scatter x1, waiting for transfers between devices, body(): lax.psum_scatter(slope_terms.astype(jnp.bfloat16), 'row', scatter_dimensi...  54 us
    all_gather x1, waiting for transfers between devices, body(): activated = lax.all_gather(active_share, 'row', axis=0, tiled=True)  30.7 us
    all_gather x1, waiting for transfers between devices, body(): scaled_all = lax.all_gather(scaled, ('rep', 'col'), axis=0, tiled=True)  27.6 us
    reduce_scatter x1, waiting for transfers between devices, body(): lax.psum_scatter(output_terms.astype(jnp.bfloat16), ('rep', 'col'), scatt...  27.5 us
    dot_general x2, matrix products, first_product(): lax.dot_general(left, right, (((0,), (0,)), ((), ())), preferred_element_...  23 us
    unnamed x18, local copies, waits for them, and re-layouts  21.9 us
  transfers between devices with their start and end apart: 10, of which 9 were waited for; matrix products, arithmetic and copies ran while one was open for 21% of the time, Pallas kernels for 0%

profile of v1, /device:TPU:0, one launch (start us, length us, event | category | flops | bytes accessed | tf_op | source)
XLA Modules:
  0.0 398.0 jit_solution(986626769923125240)
XLA Ops:
  7.2 1.3 fusion.20
  9.2 0.7 compare_convert_fusion
  9.8 1.7 fusion.16
  11.6 0.7 all-gather.9.cloned.1.call-update
  12.4 27.6 %all-gather.7.cloned.1.call-done = bf16[512,1536]{1,0:T(8,128)(2,1)} async-done(((bf16[64,1536]{1,0:T(8,128)(2,1)}), bf16[512,1536]{1,0:T(8,128)(2,1)}) %all-gather.7.cloned.1.call-update) | async-done | bytes 1572880 | tf_op jit(solution)/shard_map/all_gather | solution.py:53
  40.0 9.3 %convolution_convert_fusion = bf16[512,3072]{1,0:T(8,128)(2,1)} fusion(bf16[512,1536]{1,0:T(8,128)(2,1)} %all-gather.7.cloned.1.call-done, bf16[3072,1536]{1,0:T(8,128)(2,1)} %param.7), kind=kOutput, calls=%fused_computation.1 | convolution fusion | flops 4833411072 | bytes 14155776 | tf_op jit(solution)/shard_map/dot_general | solution.py:25
  49.4 18.1 %all-gather.9.cloned.1.call-done = bf16[1,512,1536]{2,1,0:T(8,128)(2,1)} async-done(((bf16[1,64,1536]{2,1,0:T(8,128)(2,1)}), bf16[1,512,1536]{2,1,0:T(8,128)(2,1)}) %all-gather.9.cloned.1.call-update) | async-done | bytes 1572880 | tf_op jit(solution)/shard_map/all_gather | solution.py:52
  67.5 9.2 %convolution_convert_fusion.1 = bf16[512,3072]{1,0:T(8,128)(2,1)} fusion(bf16[1536,3072]{1,0:T(8,128)(2,1)} %param.6, bf16[1,512,1536]{2,1,0:T(8,128)(2,1)} %all-gather.9.cloned.1.call-done), kind=kOutput, calls=%fused_computation.2 | convolution fusion | flops 4833411072 | bytes 14155776 | tf_op jit(solution)/shard_map/dot_general | solution.py:54
  76.8 54.0 %reduce-scatter.9.cloned.1.call-done = bf16[128,3072]{1,0:T(8,128)(2,1)} async-done(((bf16[512,3072]{1,0:T(8,128)(2,1)}), bf16[128,3072]{1,0:T(8,128)(2,1)}) %reduce-scatter.9.cloned.1.call-update) | async-done | bytes 786448 | tf_op jit(solution)/shard_map/reduce_scatter | solution.py:59
  130.8 63.1 %reduce-scatter.5.cloned.1.call-done = bf16[128,3072]{1,0:T(8,128)(2,1)} async-done(((bf16[512,3072]{1,0:T(8,128)(2,1)}), bf16[128,3072]{1,0:T(8,128)(2,1)}) %reduce-scatter.5.cloned.1.call-update) | async-done | bytes 786448 | tf_op jit(solution)/shard_map/reduce_scatter | solution.py:55
  193.9 3.4 fusion.9
  197.3 0.9 collective-permute-start
  198.2 19.8 %collective-permute-done = bf16[128,3072]{1,0:T(8,128)(2,1)S(1)} collective-permute-done((bf16[128,3072]{1,0:T(8,128)(2,1)S(1)}, bf16[128,3072]{1,0:T(8,128)(2,1)S(1)}, u32[]{:S(2)}, u32[]{:S(2)}) %collective-permute-start) | collective-permute-done | bytes 786464 | tf_op jit(solution)/shard_map/ppermute | solution.py:67
  218.0 19.8 %collective-permute-done.1 = bf16[128,3072]{1,0:T(8,128)(2,1)S(1)} collective-permute-done((bf16[128,3072]{1,0:T(8,128)(2,1)S(1)}, bf16[128,3072]{1,0:T(8,128)(2,1)S(1)}, u32[]{:S(2)}, u32[]{:S(2)}) %collective-permute-start.1) | collective-permute-done | bytes 786464 | tf_op jit(solution)/shard_map/ppermute | solution.py:67
  237.9 27.0 %collective-permute-done.2 = bf16[128,3072]{1,0:T(8,128)(2,1)S(1)} collective-permute-done((bf16[128,3072]{1,0:T(8,128)(2,1)S(1)}, bf16[128,3072]{1,0:T(8,128)(2,1)S(1)}, u32[]{:S(2)}, u32[]{:S(2)}) %collective-permute-start.2) | collective-permute-done | bytes 786464 | tf_op jit(solution)/shard_map/ppermute | solution.py:67
  265.0 0.1 constant_dynamic-update-slice_fusion.6
  265.1 0.1 constant_dynamic-update-slice_fusion.5
  265.2 0.1 constant_dynamic-update-slice_fusion.4
  265.2 0.1 constant_dynamic-update-slice_fusion.3
  265.3 0.1 constant_dynamic-update-slice_fusion.1
  265.4 0.1 constant_dynamic-update-slice_fusion
  265.5 2.7 copy-done.2
  268.2 9.1 %convolution_convert_fusion.2 = bf16[512,1536]{1,0:T(8,128)(2,1)} fusion(bf16[1536,3072]{1,0:T(8,128)(2,1)} %param.6, bf16[1024,3072]{1,0:T(8,128)(2,1)S(1)} %constant_dynamic-update-slice_fusion, s32[]{:T(128)S(6)} %select_n.29), kind=kOutput, calls=%fused_computation.10 | convolution fusion | flops 4832624640 | bytes 14155780 | tf_op jit(solution)/shard_map/dot_general | solution.py:25
  277.3 0.2 reduce-scatter.7.cloned.1.call-start
  277.5 30.7 %all-gather.5.cloned.1.call-done = bf16[512,3072]{1,0:T(8,128)(2,1)} async-done(((bf16[128,3072]{1,0:T(8,128)(2,1)}), bf16[512,3072]{1,0:T(8,128)(2,1)}) %all-gather.5.cloned.1.call-update) | async-done | bytes 3145744 | tf_op jit(solution)/shard_map/all_gather | solution.py:63
  308.2 10.3 %convolution_convert_fusion.3 = bf16[512,1536]{1,0:T(8,128)(2,1)} fusion(bf16[512,3072]{1,0:T(8,128)(2,1)} %all-gather.5.cloned.1.call-done, bf16[3072,1536]{1,0:T(8,128)(2,1)} %param.7), kind=kOutput, calls=%fused_computation.11 | convolution fusion | flops 4832624640 | bytes 14155776 | tf_op jit(solution)/shard_map/dot_general | solution.py:71
  318.4 11.6 %convolution_bitcast_fusion = f32[1536,3072]{0,1:T(8,128)} fusion(bf16[1024,3072]{1,0:T(8,128)(2,1)} %copy-done.2, s32[]{:T(128)S(6)} %select_n.29, bf16[1,512,1536]{2,1,0:T(8,128)(2,1)S(1)} %copy-done.4), kind=kOutput, calls=%fused_computation | convolution fusion | flops 4831838208 | bytes 23592964 | tf_op jit(solution)/shard_map/dot_general | solution.py:31
  330.0 18.8 %copy.9 = f32[1536,3072]{1,0:T(8,128)} copy(f32[1536,3072]{0,1:T(8,128)} %convolution_bitcast_fusion) | data formatting | bytes 37748736
  348.8 11.5 %fusion.23 = f32[3072,1536]{1,0:T(8,128)} fusion(bf16[512,3072]{1,0:T(8,128)(2,1)} %all-gather.5.cloned.1.call-done, bf16[512,1536]{1,0:T(8,128)(2,1)S(1)} %copy-done.3), kind=kOutput, calls=%fused_computation.52 | convolution fusion | flops 4831838208 | bytes 23592960 | tf_op jit(solution)/shard_map/dot_general | solution.py:31
  360.3 1.8 fusion.18
  362.0 27.5 %reduce-scatter.7.cloned.1.call-done = bf16[64,1536]{1,0:T(8,128)(2,1)} async-done(((bf16[512,1536]{1,0:T(8,128)(2,1)}), bf16[64,1536]{1,0:T(8,128)(2,1)}) %reduce-scatter.7.cloned.1.call-update) | async-done | bytes 196624 | tf_op jit(solution)/shard_map/reduce_scatter | solution.py:72
  389.5 1.6 fusion.19
  (26 shorter events, 0.5 us)
Async XLA Ops:
  7.2 32.9 %all-gather.7.cloned.1.call-start = ((), (), s32[]{:S(2)}) async-start(), calls=%async_computation.7 | async-start | bytes 1769472 | tf_op jit(solution)/shard_map/all_gather | solution.py:53
  11.6 55.9 %all-gather.9.cloned.1.call-start = ((), (), s32[]{:S(2)}) async-start(), calls=%async_computation.10 | async-start | bytes 1769472 | tf_op jit(solution)/shard_map/all_gather | solution.py:52
  12.3 118.5 %reduce-scatter.9.cloned.1.call-start = ((), (), s32[]{:S(2)}) async-start(), calls=%async_computation.8 | async-start | bytes 3932160 | tf_op jit(solution)/shard_map/reduce_scatter | solution.py:59
  49.3 144.6 %reduce-scatter.5.cloned.1.call-start = ((), (), s32[]{:S(2)}) async-start(), calls=%async_computation.4 | async-start | bytes 3932160 | tf_op jit(solution)/shard_map/reduce_scatter | solution.py:55
  76.7 231.4 %all-gather.5.cloned.1.call-start = ((), (), s32[]{:S(2)}) async-start(), calls=%async_computation.5 | async-start | bytes 3932160 | tf_op jit(solution)/shard_map/all_gather | solution.py:63
  197.3 20.7 %collective-permute-start = (bf16[128,3072]{1,0:T(8,128)(2,1)S(1)}, bf16[128,3072]{1,0:T(8,128)(2,1)S(1)}, u32[]{:S(2)}, u32[]{:S(2)}) collective-permute-start(bf16[128,3072]{1,0:T(8,128)(2,1)S(1)} %get-tuple-element.10), channel_id=1, source_target_pairs={{0,2},{2,4},{4,6},{6,0},{1,3},{3,5},{5,7},{7,1},{8,10},{10,12},{12... | collective-permute-start | bytes 2359304 | tf_op jit(solution)/shard_map/ppermute | solution.py:67
  218.0 19.8 %collective-permute-start.1 = (bf16[128,3072]{1,0:T(8,128)(2,1)S(1)}, bf16[128,3072]{1,0:T(8,128)(2,1)S(1)}, u32[]{:S(2)}, u32[]{:S(2)}) collective-permute-start(bf16[128,3072]{1,0:T(8,128)(2,1)S(1)} %collective-permute-done), channel_id=1, source_target_pairs={{0,2},{2,4},{4,6},{6,0},{1,3},{3,5},{5,7},{7,1},{8,10},{10,12},{12... | collective-permute-start | bytes 2359304 | tf_op jit(solution)/shard_map/ppermute | solution.py:67
  237.8 27.1 %collective-permute-start.2 = (bf16[128,3072]{1,0:T(8,128)(2,1)S(1)}, bf16[128,3072]{1,0:T(8,128)(2,1)S(1)}, u32[]{:S(2)}, u32[]{:S(2)}) collective-permute-start(bf16[128,3072]{1,0:T(8,128)(2,1)S(1)} %collective-permute-done.1), channel_id=1, source_target_pairs={{0,2},{2,4},{4,6},{6,0},{1,3},{3,5},{5,7},{7,1},{8,10},{10,12},{12... | collective-permute-start | bytes 2359304 | tf_op jit(solution)/shard_map/ppermute | solution.py:67
  237.9 122.4 %reduce-scatter.11.cloned.1.call-start = ((), (), s32[]{:S(2)}) async-start(), calls=%async_computation.9 | async-start | bytes 1769472 | tf_op jit(solution)/shard_map/reduce_scatter | solution.py:78
  265.5 2.7 copy-start.2
  277.3 41.2 %copy-start.4 = (bf16[1,512,1536]{2,1,0:T(8,128)(2,1)S(1)}, bf16[1,512,1536]{2,1,0:T(8,128)(2,1)}, u32[]{:S(2)}) copy-start(bf16[1,512,1536]{2,1,0:T(8,128)(2,1)} %all-gather.9.cloned.1.call-done) | copy-start | bytes 4718596
  277.3 112.3 %reduce-scatter.7.cloned.1.call-start = ((), (), s32[]{:S(2)}) async-start(), calls=%async_computation.6 | async-start | bytes 1769472 | tf_op jit(solution)/shard_map/reduce_scatter | solution.py:72
  330.0 18.8 %copy-start.3 = (bf16[512,1536]{1,0:T(8,128)(2,1)S(1)}, bf16[512,1536]{1,0:T(8,128)(2,1)}, u32[]{:S(2)}) copy-start(bf16[512,1536]{1,0:T(8,128)(2,1)} %all-gather.7.cloned.1.call-done) | copy-start | bytes 4718596
  348.8 11.5 %copy-start = (bf16[1,64,1536]{2,1,0:T(8,128)(2,1)S(1)}, bf16[1,64,1536]{2,1,0:T(8,128)(2,1)}, u32[]{:S(2)}) copy-start(bf16[1,64,1536]{2,1,0:T(8,128)(2,1)} %param.8) | copy-start | bytes 589828
  348.8 40.7 %copy-start.1 = (bf16[1,64,1536]{2,1,0:T(8,128)(2,1)S(1)}, bf16[1,64,1536]{2,1,0:T(8,128)(2,1)}, u32[]{:S(2)}) copy-start(bf16[1,64,1536]{2,1,0:T(8,128)(2,1)} %param.5) | copy-start | bytes 589828
Sparse Core Ops, SparseCore 0:
  11.7 28.2 all-gather.6
  41.9 25.5 all-gather.8
  70.4 60.3 reduce-scatter.8
  133.5 60.3 reduce-scatter.4
  238.0 70.1 all-gather.4
  311.3 36.5 reduce-scatter.10
  351.2 38.3 reduce-scatter.6
